TPU v7x, 32 devices: a whole 2x2x4 slice. The times are simulated.
32 devices in a mesh: seq: 8 (over z, core), head: 4 (over y, x).
Axes of the slice: x: 2, y: 2, z: 4, core: 2. Of those that a mesh axis runs over, the one named last changes fastest.
Arguments:
- tokens: bfloat16 [4096, 2304], P(('seq', 'head')), may hold values from -6 to 6
- in_gain: float32 [2304], replicated, may hold values from 0.5 to 1.5
- out_gain: float32 [2304], replicated, may hold values from 0.5 to 1.5
- query_weight: bfloat16 [2304, 2048], P(None, 'head'), may hold values from -1.25 to 1.25
- keyval_weight: bfloat16 [2304, 2048], replicated, may hold values from -0.125 to 0.125
- out_weight: bfloat16 [2048, 2304], P('head'), may hold values from -0.125 to 0.125
- cache_entries: bfloat16 [4, 2048, 512], P(None, 'seq'), may hold values from -6 to 6
- segment_ids: int32 [4096], P('seq'), may hold values from -1 to 63, as said below
- cache_lengths: int32 [64], replicated, may hold values from 0 to 512, as said below
- block_owners: int32 [128], P('seq'), may hold values from -1 to 63, as said below
Outputs:
- layer_out: bfloat16 [4096, 2304], P(('seq', 'head'))
Inputs may be any that keep to these rules, and one draw needn't show every extreme that they name: `segment_ids`: valid slots come first and their ids never fall; every id from 0 to 63 has at least one slot; padding slots, marked -1, fill the end of the stream; exactly one segment has 2048 slots and none has more. `block_owners`: the segment that owns each cache block, or -1 for a free block; a segment's cache fills its blocks in the order of their indices; no segment owns more than 32 blocks. `cache_lengths`: zero for a segment without blocks, and some segment has none; otherwise more than 16 times one less than its number of blocks and at most 16 times that number; exactly one segment holds 512 rows.
All inputs are finite; a program needn't handle non-finite values.
Results may differ from a plain program's by a relative error of at most 0.012.
Values may be sent and summed in bfloat16 or wider, within the bound.
A program may use at most 128 MiB of HBM per device.

v0:
```python
import math
import jax
import jax.numpy as jnp
from jax import lax
from jax.sharding import PartitionSpec as P

QH = 8
KVH = 4
HD = 256
NSEG = 64
BLK = 16
EPSILON = 1e-06
SOFT_CAP = 50.0


def carried_in(array, axis, combine, identity):
    devices, position = (lax.axis_size(axis), lax.axis_index(axis))
    everything = jax.tree.map(lambda part: lax.all_gather(part, axis), array)
    start = jax.tree.map(
        lambda part, zero: jnp.broadcast_to(jnp.asarray(zero, part.dtype), part.shape),
        array,
        identity,
    )

    def hop(k, before):
        reached = k < position
        new = combine(before, jax.tree.map(lambda part: part[k], everything))
        return jax.tree.map(lambda a, b: jnp.where(reached, a, b), new, before)

    return lax.fori_loop(0, devices, hop, start)


def rms_scale(matrix, scaling):
    matrix = matrix.astype(jnp.float32)
    mean_square = jnp.mean(matrix * matrix, axis=-1, keepdims=True)
    return matrix * lax.rsqrt(mean_square + EPSILON) * scaling


def frequencies(extent):
    return 10000.0 ** (-(jnp.arange(extent // 2, dtype=jnp.float32) * 2.0 / extent))


def rotate(vectors, angles):
    half_width = vectors.shape[-1] // 2
    leading = vectors[..., :half_width]
    trailing = vectors[..., half_width:]
    cosine = jnp.cos(angles)
    sine_part = jnp.sin(angles)
    return jnp.concatenate(
        [leading * cosine - trailing * sine_part, trailing * cosine + leading * sine_part], axis=-1
    )


def attention_fold(queries, q_seg, q_slot, key_width):
    present = q_seg >= 0

    def advance(totals, key_block):
        pair_rows, key_seg, key_slot = key_block
        numerator, denominator = totals
        scores = jnp.einsum(
            "qhd,kd->qhk", queries, pair_rows[:, :key_width], preferred_element_type=jnp.float32
        )
        scores = SOFT_CAP * jnp.tanh(scores / SOFT_CAP)
        allowed = (
            (key_seg[None, :] == q_seg[:, None])
            & (key_slot[None, :] <= q_slot[:, None])
            & present[:, None]
        )
        weights = jnp.where(allowed[:, None, :], jnp.exp(scores), 0.0)
        denominator = denominator + jnp.sum(weights, axis=-1)
        numerator = numerator + jnp.einsum(
            "qhk,kd->qhd",
            weights.astype(jnp.bfloat16),
            pair_rows[:, key_width:],
            preferred_element_type=jnp.float32,
        )
        return ((numerator, denominator), None)

    def folding(totals, portion, offset):
        pair_rows, key_seg, key_slot = portion
        row_count = pair_rows.shape[0]
        block_rows = math.gcd(row_count, 1024)
        block_count = row_count // block_rows
        blocks = (
            pair_rows.reshape(block_count, block_rows, pair_rows.shape[1]),
            key_seg.reshape(block_count, block_rows),
            key_slot.reshape(block_count, block_rows),
        )
        totals, _ = lax.scan(advance, totals, blocks)
        return totals

    return folding


def local(
    tokens,
    in_gain,
    out_gain,
    query_weight,
    keyval_weight,
    out_weight,
    cache_entries,
    segment_ids,
    cache_lengths,
    block_owners,
):
    heads_here = query_weight.shape[1] // HD
    group_size = QH // KVH
    seq_index = lax.axis_index("seq")
    head_index = lax.axis_index("head")
    shared_head = head_index * heads_here // group_size
    stream_rows = segment_ids.shape[0]
    seg_range = jnp.arange(NSEG, dtype=jnp.int32)
    matches = (segment_ids[:, None] == seg_range[None, :]).astype(jnp.int32)
    counts = jnp.sum(matches, axis=0)
    owner_match = (block_owners[:, None] == seg_range[None, :]).astype(jnp.int32)
    owned_count = jnp.sum(owner_match, axis=0)

    def add_pairs(earlier, later):
        return (earlier[0] + later[0], earlier[1] + later[1])

    empty_counts = jnp.zeros((NSEG,), jnp.int32)
    before_tokens, before_blocks = carried_in(
        (counts, owned_count), "seq", add_pairs, (empty_counts, empty_counts)
    )
    first_local = jnp.cumsum(counts) - counts
    local_slot = jnp.arange(stream_rows, dtype=jnp.int32)
    positions = (
        jnp.sum(matches * (cache_lengths + before_tokens - first_local)[None, :], axis=1)
        + local_slot
    )
    q_slot = seq_index * stream_rows + local_slot
    angles_all = positions.astype(jnp.float32)[:, None] * frequencies(HD)[None, :]
    block_rank = jnp.sum(
        owner_match * (jnp.cumsum(owner_match, axis=0) - owner_match + before_blocks[None, :]),
        axis=1,
    )
    limits = jnp.sum(owner_match * cache_lengths[None, :], axis=1)
    offsets = jnp.arange(BLK, dtype=jnp.int32)
    usable = (block_owners[:, None] >= 0) & (
        block_rank[:, None] * BLK + offsets[None, :] < limits[:, None]
    )
    cache_seg = jnp.where(usable, block_owners[:, None], -1).reshape(-1)
    cache_pairs = lax.dynamic_index_in_dim(cache_entries, shared_head, 0, keepdims=False)
    cache_slot = jnp.full((cache_seg.shape[0],), -1, jnp.int32)
    w_shared = lax.dynamic_slice_in_dim(keyval_weight, shared_head * 2 * HD, 2 * HD, 1)
    portion = lax.all_gather(tokens, "head", axis=0, tiled=True)
    row_count = portion.shape[0]
    normed = rms_scale(portion, in_gain).astype(jnp.bfloat16)
    query_rows = jnp.dot(normed, query_weight, preferred_element_type=jnp.float32).reshape(
        row_count, heads_here, HD
    )
    query_rows = (rotate(query_rows, angles_all[:, None, :]) * HD ** (-0.5)).astype(jnp.bfloat16)
    keyval = jnp.dot(normed, w_shared, preferred_element_type=jnp.float32)
    key_rows = rotate(keyval[:, :HD], angles_all).astype(jnp.bfloat16)
    value_rows = keyval[:, HD:].astype(jnp.bfloat16)
    projected = jnp.concatenate(
        [query_rows.reshape(row_count, heads_here * HD), key_rows, value_rows], axis=1
    )
    queries = projected[:, : heads_here * HD].reshape(stream_rows, heads_here, HD)
    new_pairs = projected[:, heads_here * HD :]
    folding = attention_fold(queries, segment_ids, q_slot, HD)
    start_totals = (
        jnp.zeros((stream_rows, heads_here, HD), jnp.float32),
        jnp.zeros((stream_rows, heads_here), jnp.float32),
    )
    partial_value = folding(
        start_totals,
        (
            lax.all_gather(new_pairs, "seq", axis=0, tiled=True),
            lax.all_gather(segment_ids, "seq", axis=0, tiled=True),
            lax.all_gather(q_slot, "seq", axis=0, tiled=True),
        ),
        jnp.int32(0),
    )
    numerator, denominator = folding(
        partial_value,
        (
            lax.all_gather(cache_pairs, "seq", axis=0, tiled=True),
            lax.all_gather(cache_seg, "seq", axis=0, tiled=True),
            lax.all_gather(cache_slot, "seq", axis=0, tiled=True),
        ),
        jnp.int32(0),
    )
    present = segment_ids >= 0
    safe = jnp.where(present[:, None], denominator, 1.0)
    attended = jnp.where(present[:, None, None], numerator / safe[:, :, None], 0.0)
    attended = attended.astype(jnp.bfloat16).reshape(stream_rows, heads_here * HD)
    branch = lax.psum_scatter(
        jnp.dot(attended, out_weight, preferred_element_type=jnp.float32),
        "head",
        scatter_dimension=0,
        tiled=True,
    )
    return (tokens.astype(jnp.float32) + rms_scale(branch, out_gain)).astype(jnp.bfloat16)


def solution(mesh):
    in_specs = (
        P(("seq", "head"), None),
        P(),
        P(),
        P(None, "head"),
        P(),
        P("head", None),
        P(None, "seq", None),
        P("seq"),
        P(),
        P("seq"),
    )
    out_specs = P(("seq", "head"), None)
    return jax.shard_map(local, mesh=mesh, in_specs=in_specs, out_specs=out_specs, check_vma=False)
```

profile of v0, /device:TPU:0, one launch (start us, length us, event | category | flops | bytes accessed | tf_op | source)
XLA Modules:
  0.0 246.8 jit_solution(8027556891641300505)
XLA Ops:
  6.5 0.7 all-gather.10.cloned.1.call-update
  7.4 1.2 dynamic-slice
  9.2 0.8 convert_reduce_fusion
  10.0 0.2 dynamic-update-slice
  10.2 0.7 fusion.40
  11.0 0.2 dynamic-update-slice.1
  11.2 10.6 %all-reduce.2 = (s32[512]{0:T(512)S(1)}, s32[512]{0:T(512)S(1)}) all-reduce(s32[512]{0:T(512)S(1)} %dynamic-update-slice, s32[512]{0:T(512)S(1)} %dynamic-update-slice.1), channel_id=2, replica_groups=mesh['seq'=8,'head'=4] {'seq'}, use_global_device_ids=true, to_apply=%add | all-reduce | flops 1024 | bytes 8192
  22.2 0.1 reduce.2
  22.3 0.3 while.44
  22.6 0.7 subtract_subtract_fusion
  23.3 0.8 select_reduce_fusion
  24.1 25.3 %all-gather.10.cloned.1.call-done = bf16[512,2304]{1,0:T(8,128)(2,1)} async-done(((bf16[128,2304]{1,0:T(8,128)(2,1)}), bf16[512,2304]{1,0:T(8,128)(2,1)}) %all-gather.10.cloned.1.call-update) | async-done | bytes 2359312 | tf_op jit(solution)/shard_map/all_gather | solution.py:147
  49.4 2.2 fusion.28
  51.6 3.9 %fusion.31 = f32[512,512]{0,1:T(8,128)S(1)} fusion(bf16[2304,2048]{1,0:T(8,128)(2,1)} %param.20, s32[]{:T(128)S(6)} %select_n.68, bf16[512,2304]{1,0:T(8,128)(2,1)} %all-gather.10.cloned.1.call-done, f32[2304]{0:T(1024)} %param.17, f32[512]{0:T(512)S(1)} %add_rsqrt_fusion), kind=kOutput, calls=%fused_computation.45 | convolution fusion | flops 1212678144 | bytes 5781508 | tf_op jit(solution)/shard_map/dot_general | solution.py:154
  55.6 1.2 multiply_cosine_fusion
  56.8 0.8 pad_maximum_fusion
  57.7 1.7 constant_dynamic-slice_fusion.3
  59.6 12.9 %all-gather.4 = s32[8,1,512]{2,1,0:T(1,128)S(1)} all-gather(s32[1,1,512]{2,1,0:T(1,128)S(1)} %bitcast.98), channel_id=1, replica_groups=mesh['seq'=8,'head'=4] {'seq'}, dimensions={0}, use_global_device_ids=true | all-gather | bytes 18432 | tf_op jit(solution)/shard_map/all_gather | solution.py:172
  72.5 12.9 %all-gather.3 = s32[8,1,512]{2,1,0:T(1,128)S(1)} all-gather(s32[1,1,512]{2,1,0:T(1,128)S(1)} %bitcast.97), channel_id=1, replica_groups=mesh['seq'=8,'head'=4] {'seq'}, dimensions={0}, use_global_device_ids=true | all-gather | bytes 18432 | tf_op jit(solution)/shard_map/all_gather | solution.py:171
  85.5 0.2 select_reduce_fusion.2
  85.9 9.6 %all-gather.5 = s32[8,1,256]{2,1,0:T(1,128)S(1)} all-gather(s32[1,1,256]{2,1,0:T(1,128)S(1)} %reshape.296), channel_id=1, replica_groups=mesh['seq'=8,'head'=4] {'seq'}, dimensions={0}, use_global_device_ids=true | all-gather | bytes 9216 | tf_op jit(solution)/shard_map/all_gather | solution.py:180
  95.5 0.8 copy.41
  96.3 0.8 copy.43
  97.1 3.9 %fusion.34 = f32[512,512]{0,1:T(8,128)S(1)} fusion(bf16[2304,512]{1,0:T(8,128)(2,1)} %param.19, bf16[512,2304]{1,0:T(8,128)(2,1)} %all-gather.10.cloned.1.call-done, f32[2304]{0:T(1024)S(1)} %copy-done.9, f32[512]{0:T(512)S(1)} %add_rsqrt_fusion), kind=kOutput, calls=%fused_computation.52 | convolution fusion | flops 1212678144 | bytes 5778432 | tf_op jit(solution)/shard_map/dot_general | solution.py:150
  101.0 0.9 fusion.42
  101.9 0.2 copy.49
  102.1 1.2 copy.50
  103.4 1.1 multiply_subtract_fusion
  104.5 0.9 fusion.33
  105.4 6.5 %copy.48 = bf16[4096,512]{1,0:T(8,128)(2,1)} copy(bf16[4096,512]{0,1:T(8,128)(2,1)} %all-gather.12.cloned.1.call-done) | data formatting | bytes 8388608
  111.8 48.7 %while.45 = (s32[]{:T(128)}, f32[512,2,256]{2,0,1:T(8,128)}, f32[512,2]{0,1:T(2,128)S(1)}, s32[4,1024]{1,0:T(4,128)S(1)}, s32[512]{0:T(512)S(1)}, /*index=5*/s32...) while((s32[]{:T(128)}, f32[512,2,256]{2,0,1:T(8,128)}, ...), condition=%wide.region_9.10_spmd.clone, body=%wide.region_7.9_spmd.clone.sunk | while | flops 1084753408 | bytes 17873576 | solution.py:89
  111.9 1.1 and_and_fusion.5
  112.9 1.5 dynamic-slice_bitcast_fusion.5
  114.5 4.5 %fusion.63 = (f32[512,2]{0,1:T(2,128)S(1)}, f32[1024,512,2]{1,0,2:T(8,128)}) fusion(pred[512,1024]{0,1:T(8,128)(4,1)S(1)} %and_and_fusion.5, bf16[512,2,256]{2,0,1:T(8,128)(2,1)} %get-tuple-element.669, bf16[1024,512]{1,0:T(8,128)(2,1)S(1)} %dynamic-slice_bitcast_fusion.5), kind=kOutput, calls=%fused_computation.23.clone.1 | convolution fusion | flops 541064192 | bytes 5771264 | tf_op jit(solution)/shard_map/while/body/eval_jaxpr/qhd,kd->qhk/dot_general | solution.py:60
  119.0 4.8 %fusion.64 = f32[512,2,256]{2,0,1:T(8,128)} fusion(f32[1024,512,2]{1,0,2:T(8,128)} %get-tuple-element.611, pred[512,1024]{0,1:T(8,128)(4,1)} %copy-done.1, f32[512,2,256]{2,0,1:T(8,128)} %get-tuple-element.650, bf16[1024,512]{1,0:T(8,128)(2,1)S(1)} %dynamic-slice_bitcast_fusion.5, pred[]{:T(512)S(6)} %compare.9), kind=kOutput, calls=%fused_computation.28.clone.1 | convolution fusion | flops 541589504 | bytes 7340033 | tf_op jit(solution)/shard_map/while/body/eval_jaxpr/qhk,kd->qhd/dot_general | solution.py:71
  123.9 1.1 and_and_fusion.5
  124.9 1.5 dynamic-slice_bitcast_fusion.5
  126.4 4.5 %fusion.63 = (f32[512,2]{0,1:T(2,128)S(1)}, f32[1024,512,2]{1,0,2:T(8,128)}) fusion(pred[512,1024]{0,1:T(8,128)(4,1)S(1)} %and_and_fusion.5, bf16[512,2,256]{2,0,1:T(8,128)(2,1)} %get-tuple-element.669, bf16[1024,512]{1,0:T(8,128)(2,1)S(1)} %dynamic-slice_bitcast_fusion.5), kind=kOutput, calls=%fused_computation.23.clone.1 | convolution fusion | flops 541064192 | bytes 5771264 | tf_op jit(solution)/shard_map/while/body/eval_jaxpr/qhd,kd->qhk/dot_general | solution.py:60
  131.0 5.1 %fusion.64 = f32[512,2,256]{2,0,1:T(8,128)} fusion(f32[1024,512,2]{1,0,2:T(8,128)} %get-tuple-element.611, pred[512,1024]{0,1:T(8,128)(4,1)} %copy-done.1, f32[512,2,256]{2,0,1:T(8,128)} %get-tuple-element.650, bf16[1024,512]{1,0:T(8,128)(2,1)S(1)} %dynamic-slice_bitcast_fusion.5, pred[]{:T(512)S(6)} %compare.9), kind=kOutput, calls=%fused_computation.28.clone.1 | convolution fusion | flops 541589504 | bytes 7340033 | tf_op jit(solution)/shard_map/while/body/eval_jaxpr/qhk,kd->qhd/dot_general | solution.py:71
  136.1 1.1 and_and_fusion.5
  137.2 1.5 dynamic-slice_bitcast_fusion.5
  138.7 4.5 %fusion.63 = (f32[512,2]{0,1:T(2,128)S(1)}, f32[1024,512,2]{1,0,2:T(8,128)}) fusion(pred[512,1024]{0,1:T(8,128)(4,1)S(1)} %and_and_fusion.5, bf16[512,2,256]{2,0,1:T(8,128)(2,1)} %get-tuple-element.669, bf16[1024,512]{1,0:T(8,128)(2,1)S(1)} %dynamic-slice_bitcast_fusion.5), kind=kOutput, calls=%fused_computation.23.clone.1 | convolution fusion | flops 541064192 | bytes 5771264 | tf_op jit(solution)/shard_map/while/body/eval_jaxpr/qhd,kd->qhk/dot_general | solution.py:60
  143.2 5.1 %fusion.64 = f32[512,2,256]{2,0,1:T(8,128)} fusion(f32[1024,512,2]{1,0,2:T(8,128)} %get-tuple-element.611, pred[512,1024]{0,1:T(8,128)(4,1)} %copy-done.1, f32[512,2,256]{2,0,1:T(8,128)} %get-tuple-element.650, bf16[1024,512]{1,0:T(8,128)(2,1)S(1)} %dynamic-slice_bitcast_fusion.5, pred[]{:T(512)S(6)} %compare.9), kind=kOutput, calls=%fused_computation.28.clone.1 | convolution fusion | flops 541589504 | bytes 7340033 | tf_op jit(solution)/shard_map/while/body/eval_jaxpr/qhk,kd->qhd/dot_general | solution.py:71
  148.4 1.1 and_and_fusion.5
  149.4 1.5 dynamic-slice_bitcast_fusion.5
  150.9 4.5 %fusion.63 = (f32[512,2]{0,1:T(2,128)S(1)}, f32[1024,512,2]{1,0,2:T(8,128)}) fusion(pred[512,1024]{0,1:T(8,128)(4,1)S(1)} %and_and_fusion.5, bf16[512,2,256]{2,0,1:T(8,128)(2,1)} %get-tuple-element.669, bf16[1024,512]{1,0:T(8,128)(2,1)S(1)} %dynamic-slice_bitcast_fusion.5), kind=kOutput, calls=%fused_computation.23.clone.1 | convolution fusion | flops 541064192 | bytes 5771264 | tf_op jit(solution)/shard_map/while/body/eval_jaxpr/qhd,kd->qhk/dot_general | solution.py:60
  155.5 5.1 %fusion.64 = f32[512,2,256]{2,0,1:T(8,128)} fusion(f32[1024,512,2]{1,0,2:T(8,128)} %get-tuple-element.611, pred[512,1024]{0,1:T(8,128)(4,1)} %copy-done.1, f32[512,2,256]{2,0,1:T(8,128)} %get-tuple-element.650, bf16[1024,512]{1,0:T(8,128)(2,1)S(1)} %dynamic-slice_bitcast_fusion.5, pred[]{:T(512)S(6)} %compare.9), kind=kOutput, calls=%fused_computation.28.clone.1 | convolution fusion | flops 541589504 | bytes 7340033 | tf_op jit(solution)/shard_map/while/body/eval_jaxpr/qhk,kd->qhd/dot_general | solution.py:71
  160.6 14.8 %while.43 = (s32[]{:T(128)}, f32[512,2,256]{2,0,1:T(8,128)}, f32[512,2]{0,1:T(2,128)S(1)}, s32[2,1024]{1,0:T(2,128)S(1)}, s32[512]{0:T(512)S(1)}, /*index=5*/pre...) while((s32[]{:T(128)}, f32[512,2,256]{2,0,1:T(8,128)}, ...), condition=%wide.region_15.16_spmd.clone, body=%wide.region_13.15_spmd.clone.sunk | while | flops 1083966464 | bytes 24149672 | solution.py:89
  160.6 0.5 and_and_fusion.4
  161.1 1.3 dynamic-slice_bitcast_fusion.4
  162.4 2.7 %fusion.59 = (f32[512,2]{0,1:T(2,128)S(1)}, f32[1024,512,2]{1,0,2:T(8,128)S(1)}) fusion(pred[512,1024]{0,1:T(8,128)(4,1)S(1)} %and_and_fusion.4, bf16[512,2,256]{2,0,1:T(8,128)(2,1)} %get-tuple-element.700, bf16[1024,512]{1,0:T(8,128)(2,1)S(1)} %dynamic-slice_bitcast_fusion.4), kind=kOutput, calls=%fused_computation.3.clone.1 | convolution fusion | flops 541064192 | bytes 5771264 | tf_op jit(solution)/shard_map/while/body/eval_jaxpr/qhd,kd->qhk/dot_general | solution.py:60
  165.2 1.8 fusion.60
  167.1 0.9 copy-done.4
  168.0 0.5 and_and_fusion.4
  168.5 1.3 dynamic-slice_bitcast_fusion.4
  169.8 2.7 %fusion.59 = (f32[512,2]{0,1:T(2,128)S(1)}, f32[1024,512,2]{1,0,2:T(8,128)S(1)}) fusion(pred[512,1024]{0,1:T(8,128)(4,1)S(1)} %and_and_fusion.4, bf16[512,2,256]{2,0,1:T(8,128)(2,1)} %get-tuple-element.700, bf16[1024,512]{1,0:T(8,128)(2,1)S(1)} %dynamic-slice_bitcast_fusion.4), kind=kOutput, calls=%fused_computation.3.clone.1 | convolution fusion | flops 541064192 | bytes 5771264 | tf_op jit(solution)/shard_map/while/body/eval_jaxpr/qhd,kd->qhk/dot_general | solution.py:60
  172.6 1.9 fusion.60
  174.5 0.9 copy-done.4
  175.4 1.6 copy.45
  177.0 0.1 select_convert_fusion
  177.1 3.5 %fusion.43 = f32[512,2304]{1,0:T(8,128)} fusion(bf16[512,512]{0,1:T(8,128)(2,1)S(1)} %bitcast.92, bf16[512,2304]{1,0:T(8,128)(2,1)S(1)} %copy-done), kind=kOutput, calls=%fused_computation.85 | convolution fusion | flops 1207959552 | bytes 7602176 | tf_op jit(solution)/shard_map/dot_general | solution.py:190
  180.7 55.8 %reduce-scatter.2.cloned.1.call-done = f32[128,2304]{1,0:T(8,128)} async-done(((f32[512,2304]{1,0:T(8,128)}), f32[128,2304]{1,0:T(8,128)}) %reduce-scatter.2.cloned.1.call-update) | async-done | bytes 1179664 | tf_op jit(solution)/shard_map/reduce_scatter | solution.py:189
  236.5 1.4 multiply_reduce_fusion
  237.9 2.3 add_convert_fusion
  (93 shorter events, 1.4 us)
Async XLA Ops:
  6.5 170.6 %copy-start = (bf16[512,2304]{1,0:T(8,128)(2,1)S(1)}, bf16[512,2304]{1,0:T(8,128)(2,1)}, u32[]{:S(2)}) copy-start(bf16[512,2304]{1,0:T(8,128)(2,1)} %param.21) | copy-start | bytes 7077892
  6.5 42.9 %all-gather.10.cloned.1.call-start = ((), (), s32[]{:S(2)}) async-start(), calls=%async_computation.1 | async-start | bytes 2949120 | tf_op jit(solution)/shard_map/all_gather | solution.py:147
  7.3 98.1 %all-gather.12.cloned.1.call-start = ((), (), s32[]{:S(2)}) async-start(), calls=%async_computation.2 | async-start | bytes 4718592 | tf_op jit(solution)/shard_map/all_gather | solution.py:170
  55.5 3.9 %copy-start.5 = (s32[512]{0:T(512)S(1)}, s32[512]{0:T(512)}, u32[]{:S(2)}) copy-start(s32[512]{0:T(512)} %param.23) | copy-start | bytes 6148
  55.6 4.0 %copy-start.7 = (s32[16]{0:T(128)S(1)}, s32[16]{0:T(128)}, u32[]{:S(2)}) copy-start(s32[16]{0:T(128)} %param.25) | copy-start | bytes 196
  55.6 29.9 %copy-start.8 = (s32[64]{0:T(128)S(1)}, s32[64]{0:T(128)}, u32[]{:S(2)}) copy-start(s32[64]{0:T(128)} %param.24) | copy-start | bytes 772
  55.6 41.6 %copy-start.9 = (f32[2304]{0:T(1024)S(1)}, f32[2304]{0:T(1024)}, u32[]{:S(2)}) copy-start(f32[2304]{0:T(1024)} %param.17) | copy-start | bytes 27652
  57.7 102.9 %all-gather.14.cloned.1.call-start = ((), (), s32[]{:S(2)}) async-start(), calls=%async_computation.4 | async-start | bytes 2359296 | tf_op jit(solution)/shard_map/all_gather | solution.py:179
  59.4 177.1 %reduce-scatter.2.cloned.1.call-start = ((), (), s32[]{:S(2)}) async-start(), calls=%async_computation.3 | async-start | bytes 5898240 | tf_op jit(solution)/shard_map/reduce_scatter | solution.py:189
  112.9 6.1 %copy-start.1 = (pred[512,1024]{0,1:T(8,128)(4,1)}, pred[512,1024]{0,1:T(8,128)(4,1)S(1)}, u32[]{:S(2)}) copy-start(pred[512,1024]{0,1:T(8,128)(4,1)S(1)} %and_and_fusion.5) | copy-start | bytes 1572868 | tf_op jit(solution)/shard_map/while
  124.9 6.0 %copy-start.1 = (pred[512,1024]{0,1:T(8,128)(4,1)}, pred[512,1024]{0,1:T(8,128)(4,1)S(1)}, u32[]{:S(2)}) copy-start(pred[512,1024]{0,1:T(8,128)(4,1)S(1)} %and_and_fusion.5) | copy-start | bytes 1572868 | tf_op jit(solution)/shard_map/while
  137.2 6.0 %copy-start.1 = (pred[512,1024]{0,1:T(8,128)(4,1)}, pred[512,1024]{0,1:T(8,128)(4,1)S(1)}, u32[]{:S(2)}) copy-start(pred[512,1024]{0,1:T(8,128)(4,1)S(1)} %and_and_fusion.5) | copy-start | bytes 1572868 | tf_op jit(solution)/shard_map/while
  149.4 6.0 %copy-start.1 = (pred[512,1024]{0,1:T(8,128)(4,1)}, pred[512,1024]{0,1:T(8,128)(4,1)S(1)}, u32[]{:S(2)}) copy-start(pred[512,1024]{0,1:T(8,128)(4,1)S(1)} %and_and_fusion.5) | copy-start | bytes 1572868 | tf_op jit(solution)/shard_map/while
  162.4 2.7 %copy-start.3 = (f32[512,2,256]{2,0,1:T(8,128)S(1)}, f32[512,2,256]{2,0,1:T(8,128)}, u32[]{:S(2)}) copy-start(f32[512,2,256]{2,0,1:T(8,128)} %get-tuple-element.684) | copy-start | bytes 3145732 | tf_op jit(solution)/shard_map/while
  167.0 1.0 copy-start.4
  169.8 2.7 %copy-start.3 = (f32[512,2,256]{2,0,1:T(8,128)S(1)}, f32[512,2,256]{2,0,1:T(8,128)}, u32[]{:S(2)}) copy-start(f32[512,2,256]{2,0,1:T(8,128)} %get-tuple-element.684) | copy-start | bytes 3145732 | tf_op jit(solution)/shard_map/while
  174.4 1.0 copy-start.4
  180.7 57.2 %copy-start.2 = (bf16[128,2304]{1,0:T(8,128)(2,1)S(1)}, bf16[128,2304]{1,0:T(8,128)(2,1)}, u32[]{:S(2)}) copy-start(bf16[128,2304]{1,0:T(8,128)(2,1)} %param.16) | copy-start | bytes 1769476
  180.7 57.3 %copy-start.6 = (f32[2304]{0:T(1024)S(1)}, f32[2304]{0:T(1024)}, u32[]{:S(2)}) copy-start(f32[2304]{0:T(1024)} %param.18) | copy-start | bytes 27652
Sparse Core Ops, SparseCore 0:
  9.2 40.1 all-gather.9
  57.8 47.2 all-gather.11
  106.7 27.8 all-gather.13
  180.8 55.6 reduce-scatter.1
where the time goes:
time: 248 us; the launch traced here: 247 us
  waiting for transfers between devices  81.9 us (33%)
  matrix products  58.7 us (24%)
  blocking collectives  45.9 us (19%)
  local copies, waits for them, and re-layouts  26.4 us (11%)
  other arithmetic  19.2 us (8%)
  between operations  14 us (6%)
    reduce_scatter x1, waiting for transfers between devices, local(): lax.psum_scatter(jnp.dot(attended, out_weight, preferred_element_type=jnp...  55.8 us
    all_gather x1, waiting for transfers between devices, local(): portion = lax.all_gather(tokens, 'head', axis=0, tiled=True)  25.3 us
    dot_general x6, matrix products, advance(): jnp.einsum('qhk,kd->qhd', weights.astype(jnp.bfloat16), pair_rows[:, key_...  23.7 us
    dot_general x6, matrix products, advance(): jnp.einsum('qhd,kd->qhk', queries, pair_rows[:, :key_width], preferred_el...  23.6 us
    all_gather x1, blocking collectives, local(): lax.all_gather(segment_ids, 'seq', axis=0, tiled=True)  12.9 us
    all_gather x1, blocking collectives, local(): lax.all_gather(q_slot, 'seq', axis=0, tiled=True)  12.9 us
    unnamed x1, blocking collectives  10.6 us
    unnamed x21, local copies, waits for them, and re-layouts  9.73 us
  transfers between devices with their start and end apart: 4, of which 2 were waited for; matrix products, arithmetic and copies ran while one was open for 29% of the time, Pallas kernels for 0%

commit v1 on v0

--- a/solution.py
+++ b/solution.py
@@ -144,7 +144,12 @@
     cache_pairs = lax.dynamic_index_in_dim(cache_entries, shared_head, 0, keepdims=False)
     cache_slot = jnp.full((cache_seg.shape[0],), -1, jnp.int32)
     w_shared = lax.dynamic_slice_in_dim(keyval_weight, shared_head * 2 * HD, 2 * HD, 1)
-    portion = lax.all_gather(tokens, "head", axis=0, tiled=True)
+    ring = [tokens]
+    for hop_ in range(3):
+        ring.append(lax.ppermute(ring[-1], "head", [(dev, (dev + 1) % 4) for dev in range(4)]))
+    portion = jnp.roll(
+        jnp.concatenate(ring[::-1], axis=0), (lax.axis_index("head") + 1) * ring[0].shape[0], axis=0
+    )
     row_count = portion.shape[0]
     normed = rms_scale(portion, in_gain).astype(jnp.bfloat16)
     query_rows = jnp.dot(normed, query_weight, preferred_element_type=jnp.float32).reshape(

time: 248 us -> 260 us (1.048)
  local copies, waits for them, and re-layouts: 26.4 us -> 36.5 us
  starting transfers between devices: 0.12 us -> 4.81 us
  waiting for transfers between devices: 81.9 us -> 77.8 us
    all_gather x1 -> x0, waiting for transfers between devices: 25.3 us -> none  [local(): portion = lax.all_gather(tokens, 'head', axis=0, tiled=True)]
    ppermute x0 -> x3, waiting for transfers between devices: none -> 22.3 us  [local(): lax.ppermute(ring[-1], 'head', [(dev, (dev + 1) % 4) for dev in range(4)])]
    unnamed x21 -> x36, local copies, waits for them, and re-layouts: 9.73 us -> 15.3 us
    ppermute x0 -> x3, starting transfers between devices: none -> 4.73 us  [local(): lax.ppermute(ring[-1], 'head', [(dev, (dev + 1) % 4) for dev in range(4)])]
  transfers between devices with their start and end apart: 4 -> 6, of which waited for: 2 -> 3; matrix products, arithmetic and copies ran while one was open for 29% -> 31% of each run, Pallas kernels for 0% -> 0%
where the time goes in v1:
time: 260 us; the launch traced here: 258 us
  waiting for transfers between devices  77.8 us (30%)
  matrix products  59.1 us (23%)
  blocking collectives  44.5 us (17%)
  local copies, waits for them, and re-layouts  36.5 us (14%)
  other arithmetic  21 us (8%)
  between operations  14.1 us (5%)
  starting transfers between devices  4.81 us (2%)
    reduce_scatter x1, waiting for transfers between devices, local(): lax.psum_scatter(jnp.dot(attended, out_weight, preferred_element_type=jnp...  55.4 us
    dot_general x6, matrix products, advance(): jnp.einsum('qhk,kd->qhd', weights.astype(jnp.bfloat16), pair_rows[:, key_...  23.7 us
    dot_general x6, matrix products, advance(): jnp.einsum('qhd,kd->qhk', queries, pair_rows[:, :key_width], preferred_el...  23.6 us
    ppermute x3, waiting for transfers between devices, local(): lax.ppermute(ring[-1], 'head', [(dev, (dev + 1) % 4) for dev in range(4)])  22.3 us
    unnamed x36, local copies, waits for them, and re-layouts  15.3 us
    all_gather x1, blocking collectives, local(): lax.all_gather(segment_ids, 'seq', axis=0, tiled=True)  13 us
    all_gather x1, blocking collectives, local(): lax.all_gather(q_slot, 'seq', axis=0, tiled=True)  12.8 us
    unnamed x1, blocking collectives  9.76 us
  transfers between devices with their start and end apart: 6, of which 3 were waited for; matrix products, arithmetic and copies ran while one was open for 31% of the time, Pallas kernels for 0%

profile of v1, /device:TPU:0, one launch (start us, length us, event | category | flops | bytes accessed | tf_op | source)
XLA Modules:
  0.0 258.2 jit_solution(16121590005140627763)
XLA Ops:
  6.5 2.9 %collective-permute-start = (bf16[128,2304]{1,0:T(8,128)(2,1)}, bf16[128,2304]{1,0:T(8,128)(2,1)S(1)}, u32[]{:S(2)}, u32[]{:S(2)}) collective-permute-start(bf16[128,2304]{1,0:T(8,128)(2,1)} %param.16), channel_id=1, source_target_pairs={{0,1},{1,2},{2,3},{3,0},{4,5},{5,6},{6,7},{7,4},{8,9},{9,10},{10,1... | collective-permute-start | bytes 1769480 | tf_op jit(solution)/shard_map/ppermute | solution.py:149
  9.5 1.2 dynamic-slice
  11.4 0.8 convert_reduce_fusion
  12.8 1.3 fusion.40
  14.1 0.9 dynamic-update-slice.1
  15.0 9.8 %all-reduce.2 = (s32[512]{0:T(512)}, s32[512]{0:T(512)}) all-reduce(s32[512]{0:T(512)S(1)} %dynamic-update-slice, s32[512]{0:T(512)S(1)} %dynamic-update-slice.1), channel_id=2, replica_groups=mesh['seq'=8,'head'=4] {'seq'}, use_global_device_ids=true, to_apply=%add | all-reduce | flops 1024 | bytes 8192
  25.5 0.8 reshape.283
  26.2 1.5 collective-permute-start.1
  28.0 13.3 %collective-permute-done.1 = bf16[128,2304]{1,0:T(8,128)(2,1)} collective-permute-done((bf16[128,2304]{1,0:T(8,128)(2,1)S(1)}, bf16[128,2304]{1,0:T(8,128)(2,1)}, u32[]{:S(2)}, u32[]{:S(2)}) %collective-permute-start.1) | collective-permute-done | bytes 589856 | tf_op jit(solution)/shard_map/ppermute | solution.py:149
  41.7 1.4 copy.39
  43.0 1.4 reduce-window.9
  44.5 0.9 reduce.2
  46.0 0.8 select_reduce_fusion
  46.8 9.0 %collective-permute-done.2 = bf16[128,2304]{1,0:T(8,128)(2,1)} collective-permute-done((bf16[128,2304]{1,0:T(8,128)(2,1)}, bf16[128,2304]{1,0:T(8,128)(2,1)}, u32[]{:S(2)}, u32[]{:S(2)}) %collective-permute-start.2) | collective-permute-done | bytes 589856 | tf_op jit(solution)/shard_map/ppermute | solution.py:149
  55.7 1.1 constant_dynamic-update-slice_fusion.7
  56.9 1.1 constant_dynamic-update-slice_fusion.6
  58.1 1.1 constant_dynamic-update-slice_fusion.3
  59.2 1.1 constant_dynamic-update-slice_fusion.2
  61.0 4.3 %fusion.31 = f32[512,512]{0,1:T(8,128)S(1)} fusion(bf16[2304,2048]{1,0:T(8,128)(2,1)} %param.20, s32[]{:T(128)S(6)} %select_n.82, f32[2304]{0:T(1024)S(1)} %copy-done.12, f32[512]{0:T(512)S(1)} %add_rsqrt_fusion, bf16[1024,2304]{1,0:T(8,128)(2,1)S(1)} %constant_dynamic-update-slice_fusion, s32[]{:T(128)S(6)} %select_n.80), kind=kOutput, calls=%fused_computation.45 | convolution fusion | flops 1212678144 | bytes 5781512 | tf_op jit(solution)/shard_map/dot_general | solution.py:159
  65.4 1.9 multiply_cosine_fusion
  67.3 0.8 pad_maximum_fusion
  68.2 1.7 constant_dynamic-slice_fusion.3
  70.1 12.8 %all-gather.4 = s32[8,1,512]{2,1,0:T(1,128)S(1)} all-gather(s32[1,1,512]{2,1,0:T(1,128)S(1)} %bitcast.98), channel_id=1, replica_groups=mesh['seq'=8,'head'=4] {'seq'}, dimensions={0}, use_global_device_ids=true | all-gather | bytes 18432 | tf_op jit(solution)/shard_map/all_gather | solution.py:177
  83.0 13.0 %all-gather.3 = s32[8,1,512]{2,1,0:T(1,128)S(1)} all-gather(s32[1,1,512]{2,1,0:T(1,128)S(1)} %bitcast.97), channel_id=1, replica_groups=mesh['seq'=8,'head'=4] {'seq'}, dimensions={0}, use_global_device_ids=true | all-gather | bytes 18432 | tf_op jit(solution)/shard_map/all_gather | solution.py:176
  96.4 8.9 %all-gather.5 = s32[8,1,256]{2,1,0:T(1,128)S(1)} all-gather(s32[1,1,256]{2,1,0:T(1,128)S(1)} %reshape.296), channel_id=1, replica_groups=mesh['seq'=8,'head'=4] {'seq'}, dimensions={0}, use_global_device_ids=true | all-gather | bytes 9216 | tf_op jit(solution)/shard_map/all_gather | solution.py:185
  105.4 3.9 %fusion.34 = f32[512,512]{0,1:T(8,128)S(1)} fusion(bf16[2304,512]{1,0:T(8,128)(2,1)} %param.19, f32[2304]{0:T(1024)S(1)} %copy-done.13, f32[512]{0:T(512)S(1)} %add_rsqrt_fusion, bf16[1024,2304]{1,0:T(8,128)(2,1)} %copy-done.4, s32[]{:T(128)S(6)} %select_n.80), kind=kOutput, calls=%fused_computation.56 | convolution fusion | flops 1212678144 | bytes 5778436 | tf_op jit(solution)/shard_map/dot_general | solution.py:155
  109.3 0.9 fusion.43
  110.4 1.2 copy.50
  111.6 1.8 copy.41
  113.4 1.8 copy.43
  115.2 1.1 multiply_subtract_fusion
  116.4 0.9 fusion.33
  117.2 6.5 %copy.48 = bf16[4096,512]{1,0:T(8,128)(2,1)} copy(bf16[4096,512]{0,1:T(8,128)(2,1)} %all-gather.9.cloned.1.call-done) | data formatting | bytes 8388608
  123.7 48.6 %while.45 = (s32[]{:T(128)}, f32[512,2,256]{2,0,1:T(8,128)}, f32[512,2]{0,1:T(2,128)S(1)}, s32[4,1024]{1,0:T(4,128)S(1)}, s32[512]{0:T(512)S(1)}, /*index=5*/s32...) while((s32[]{:T(128)}, f32[512,2,256]{2,0,1:T(8,128)}, ...), condition=%wide.region_9.10_spmd.clone, body=%wide.region_7.9_spmd.clone.sunk | while | flops 1084753408 | bytes 17873576 | solution.py:89
  123.7 1.1 and_and_fusion.5
  124.8 1.5 dynamic-slice_bitcast_fusion.5
  126.3 4.5 %fusion.64 = (f32[512,2]{0,1:T(2,128)S(1)}, f32[1024,512,2]{1,0,2:T(8,128)}) fusion(pred[512,1024]{0,1:T(8,128)(4,1)S(1)} %and_and_fusion.5, bf16[512,2,256]{2,0,1:T(8,128)(2,1)} %get-tuple-element.669, bf16[1024,512]{1,0:T(8,128)(2,1)S(1)} %dynamic-slice_bitcast_fusion.5), kind=kOutput, calls=%fused_computation.23.clone.1 | convolution fusion | flops 541064192 | bytes 5771264 | tf_op jit(solution)/shard_map/while/body/eval_jaxpr/qhd,kd->qhk/dot_general | solution.py:60
  130.9 4.8 %fusion.65 = f32[512,2,256]{2,0,1:T(8,128)} fusion(f32[1024,512,2]{1,0,2:T(8,128)} %get-tuple-element.611, pred[512,1024]{0,1:T(8,128)(4,1)} %copy-done.1, f32[512,2,256]{2,0,1:T(8,128)} %get-tuple-element.650, bf16[1024,512]{1,0:T(8,128)(2,1)S(1)} %dynamic-slice_bitcast_fusion.5, pred[]{:T(512)S(6)} %compare.10), kind=kOutput, calls=%fused_computation.28.clone.1 | convolution fusion | flops 541589504 | bytes 7340033 | tf_op jit(solution)/shard_map/while/body/eval_jaxpr/qhk,kd->qhd/dot_general | solution.py:71
  135.7 1.1 and_and_fusion.5
  136.8 1.5 dynamic-slice_bitcast_fusion.5
  138.3 4.5 %fusion.64 = (f32[512,2]{0,1:T(2,128)S(1)}, f32[1024,512,2]{1,0,2:T(8,128)}) fusion(pred[512,1024]{0,1:T(8,128)(4,1)S(1)} %and_and_fusion.5, bf16[512,2,256]{2,0,1:T(8,128)(2,1)} %get-tuple-element.669, bf16[1024,512]{1,0:T(8,128)(2,1)S(1)} %dynamic-slice_bitcast_fusion.5), kind=kOutput, calls=%fused_computation.23.clone.1 | convolution fusion | flops 541064192 | bytes 5771264 | tf_op jit(solution)/shard_map/while/body/eval_jaxpr/qhd,kd->qhk/dot_general | solution.py:60
  142.8 5.1 %fusion.65 = f32[512,2,256]{2,0,1:T(8,128)} fusion(f32[1024,512,2]{1,0,2:T(8,128)} %get-tuple-element.611, pred[512,1024]{0,1:T(8,128)(4,1)} %copy-done.1, f32[512,2,256]{2,0,1:T(8,128)} %get-tuple-element.650, bf16[1024,512]{1,0:T(8,128)(2,1)S(1)} %dynamic-slice_bitcast_fusion.5, pred[]{:T(512)S(6)} %compare.10), kind=kOutput, calls=%fused_computation.28.clone.1 | convolution fusion | flops 541589504 | bytes 7340033 | tf_op jit(solution)/shard_map/while/body/eval_jaxpr/qhk,kd->qhd/dot_general | solution.py:71
  147.9 1.1 and_and_fusion.5
  149.0 1.5 dynamic-slice_bitcast_fusion.5
  150.5 4.5 %fusion.64 = (f32[512,2]{0,1:T(2,128)S(1)}, f32[1024,512,2]{1,0,2:T(8,128)}) fusion(pred[512,1024]{0,1:T(8,128)(4,1)S(1)} %and_and_fusion.5, bf16[512,2,256]{2,0,1:T(8,128)(2,1)} %get-tuple-element.669, bf16[1024,512]{1,0:T(8,128)(2,1)S(1)} %dynamic-slice_bitcast_fusion.5), kind=kOutput, calls=%fused_computation.23.clone.1 | convolution fusion | flops 541064192 | bytes 5771264 | tf_op jit(solution)/shard_map/while/body/eval_jaxpr/qhd,kd->qhk/dot_general | solution.py:60
  155.0 5.1 %fusion.65 = f32[512,2,256]{2,0,1:T(8,128)} fusion(f32[1024,512,2]{1,0,2:T(8,128)} %get-tuple-element.611, pred[512,1024]{0,1:T(8,128)(4,1)} %copy-done.1, f32[512,2,256]{2,0,1:T(8,128)} %get-tuple-element.650, bf16[1024,512]{1,0:T(8,128)(2,1)S(1)} %dynamic-slice_bitcast_fusion.5, pred[]{:T(512)S(6)} %compare.10), kind=kOutput, calls=%fused_computation.28.clone.1 | convolution fusion | flops 541589504 | bytes 7340033 | tf_op jit(solution)/shard_map/while/body/eval_jaxpr/qhk,kd->qhd/dot_general | solution.py:71
  160.2 1.1 and_and_fusion.5
  161.2 1.5 dynamic-slice_bitcast_fusion.5
  162.7 4.5 %fusion.64 = (f32[512,2]{0,1:T(2,128)S(1)}, f32[1024,512,2]{1,0,2:T(8,128)}) fusion(pred[512,1024]{0,1:T(8,128)(4,1)S(1)} %and_and_fusion.5, bf16[512,2,256]{2,0,1:T(8,128)(2,1)} %get-tuple-element.669, bf16[1024,512]{1,0:T(8,128)(2,1)S(1)} %dynamic-slice_bitcast_fusion.5), kind=kOutput, calls=%fused_computation.23.clone.1 | convolution fusion | flops 541064192 | bytes 5771264 | tf_op jit(solution)/shard_map/while/body/eval_jaxpr/qhd,kd->qhk/dot_general | solution.py:60
  167.3 5.1 %fusion.65 = f32[512,2,256]{2,0,1:T(8,128)} fusion(f32[1024,512,2]{1,0,2:T(8,128)} %get-tuple-element.611, pred[512,1024]{0,1:T(8,128)(4,1)} %copy-done.1, f32[512,2,256]{2,0,1:T(8,128)} %get-tuple-element.650, bf16[1024,512]{1,0:T(8,128)(2,1)S(1)} %dynamic-slice_bitcast_fusion.5, pred[]{:T(512)S(6)} %compare.10), kind=kOutput, calls=%fused_computation.28.clone.1 | convolution fusion | flops 541589504 | bytes 7340033 | tf_op jit(solution)/shard_map/while/body/eval_jaxpr/qhk,kd->qhd/dot_general | solution.py:71
  172.4 14.8 %while.43 = (s32[]{:T(128)}, f32[512,2,256]{2,0,1:T(8,128)}, f32[512,2]{0,1:T(2,128)S(1)}, s32[2,1024]{1,0:T(2,128)S(1)}, s32[512]{0:T(512)S(1)}, /*index=5*/pre...) while((s32[]{:T(128)}, f32[512,2,256]{2,0,1:T(8,128)}, ...), condition=%wide.region_15.16_spmd.clone, body=%wide.region_13.15_spmd.clone.sunk | while | flops 1083966464 | bytes 24149672 | solution.py:89
  172.9 1.3 dynamic-slice_bitcast_fusion.4
  174.2 2.7 %fusion.60 = (f32[512,2]{0,1:T(2,128)S(1)}, f32[1024,512,2]{1,0,2:T(8,128)S(1)}) fusion(pred[512,1024]{0,1:T(8,128)(4,1)S(1)} %and_and_fusion.4, bf16[512,2,256]{2,0,1:T(8,128)(2,1)} %get-tuple-element.700, bf16[1024,512]{1,0:T(8,128)(2,1)S(1)} %dynamic-slice_bitcast_fusion.4), kind=kOutput, calls=%fused_computation.3.clone.1 | convolution fusion | flops 541064192 | bytes 5771264 | tf_op jit(solution)/shard_map/while/body/eval_jaxpr/qhd,kd->qhk/dot_general | solution.py:60
  177.0 1.9 fusion.61
  178.9 0.9 copy-done.6
  180.3 1.3 dynamic-slice_bitcast_fusion.4
  181.6 2.7 %fusion.60 = (f32[512,2]{0,1:T(2,128)S(1)}, f32[1024,512,2]{1,0,2:T(8,128)S(1)}) fusion(pred[512,1024]{0,1:T(8,128)(4,1)S(1)} %and_and_fusion.4, bf16[512,2,256]{2,0,1:T(8,128)(2,1)} %get-tuple-element.700, bf16[1024,512]{1,0:T(8,128)(2,1)S(1)} %dynamic-slice_bitcast_fusion.4), kind=kOutput, calls=%fused_computation.3.clone.1 | convolution fusion | flops 541064192 | bytes 5771264 | tf_op jit(solution)/shard_map/while/body/eval_jaxpr/qhd,kd->qhk/dot_general | solution.py:60
  184.4 1.9 fusion.61
  186.3 0.9 copy-done.6
  187.2 1.6 copy.45
  188.9 3.5 %fusion.44 = f32[512,2304]{1,0:T(8,128)} fusion(bf16[512,512]{0,1:T(8,128)(2,1)S(1)} %bitcast.92, bf16[512,2304]{1,0:T(8,128)(2,1)S(1)} %copy-done), kind=kOutput, calls=%fused_computation.94 | convolution fusion | flops 1207959552 | bytes 7602176 | tf_op jit(solution)/shard_map/dot_general | solution.py:195
  192.5 55.4 %reduce-scatter.2.cloned.1.call-done = f32[128,2304]{1,0:T(8,128)} async-done(((f32[512,2304]{1,0:T(8,128)}), f32[128,2304]{1,0:T(8,128)}) %reduce-scatter.2.cloned.1.call-update) | async-done | bytes 1179664 | tf_op jit(solution)/shard_map/reduce_scatter | solution.py:194
  247.9 1.4 multiply_reduce_fusion
  249.4 2.3 add_convert_fusion
  (112 shorter events, 5.8 us)
Async XLA Ops:
  6.5 182.4 %copy-start = (bf16[512,2304]{1,0:T(8,128)(2,1)S(1)}, bf16[512,2304]{1,0:T(8,128)(2,1)}, u32[]{:S(2)}) copy-start(bf16[512,2304]{1,0:T(8,128)(2,1)} %param.21) | copy-start | bytes 7077892
  6.5 51.5 %copy-start.2 = (bf16[128,2304]{1,0:T(8,128)(2,1)S(1)}, bf16[128,2304]{1,0:T(8,128)(2,1)}, u32[]{:S(2)}) copy-start(bf16[128,2304]{1,0:T(8,128)(2,1)} %param.16) | copy-start | bytes 1769476
  6.5 110.7 %all-gather.9.cloned.1.call-start = ((), (), s32[]{:S(2)}) async-start(), calls=%async_computation.1 | async-start | bytes 4718592 | tf_op jit(solution)/shard_map/all_gather | solution.py:175
  6.5 19.7 %collective-permute-start = (bf16[128,2304]{1,0:T(8,128)(2,1)}, bf16[128,2304]{1,0:T(8,128)(2,1)S(1)}, u32[]{:S(2)}, u32[]{:S(2)}) collective-permute-start(bf16[128,2304]{1,0:T(8,128)(2,1)} %param.16), channel_id=1, source_target_pairs={{0,1},{1,2},{2,3},{3,0},{4,5},{5,6},{6,7},{7,4},{8,9},{9,10},{10,1... | collective-permute-start | bytes 1769480 | tf_op jit(solution)/shard_map/ppermute | solution.py:149
  12.2 0.6 copy-start.9
  26.2 15.1 %collective-permute-start.1 = (bf16[128,2304]{1,0:T(8,128)(2,1)S(1)}, bf16[128,2304]{1,0:T(8,128)(2,1)}, u32[]{:S(2)}, u32[]{:S(2)}) collective-permute-start(bf16[128,2304]{1,0:T(8,128)(2,1)S(1)} %collective-permute-done), channel_id=1, source_target_pairs={{0,1},{1,2},{2,3},{3,0},{4,5},{5,6},{6,7},{7,4},{8,9},{9,10},{10,1... | collective-permute-start | bytes 1769480 | tf_op jit(solution)/shard_map/ppermute | solution.py:149
  41.3 14.4 %collective-permute-start.2 = (bf16[128,2304]{1,0:T(8,128)(2,1)}, bf16[128,2304]{1,0:T(8,128)(2,1)}, u32[]{:S(2)}, u32[]{:S(2)}) collective-permute-start(bf16[128,2304]{1,0:T(8,128)(2,1)} %collective-permute-done.1), channel_id=1, source_target_pairs={{0,1},{1,2},{2,3},{3,0},{4,5},{5,6},{6,7},{7,4},{8,9},{9,10},{10,1... | collective-permute-start | bytes 1769480 | tf_op jit(solution)/shard_map/ppermute | solution.py:149
  58.0 2.9 %copy-start.12 = (f32[2304]{0:T(1024)S(1)}, f32[2304]{0:T(1024)}, u32[]{:S(2)}) copy-start(f32[2304]{0:T(1024)} %param.17) | copy-start | bytes 27652
  60.4 4.9 %copy-start.4 = (bf16[1024,2304]{1,0:T(8,128)(2,1)}, bf16[1024,2304]{1,0:T(8,128)(2,1)S(1)}, u32[]{:S(2)}) copy-start(bf16[1024,2304]{1,0:T(8,128)(2,1)S(1)} %constant_dynamic-update-slice_fusion) | copy-start | bytes 14155780
  65.3 4.6 %copy-start.7 = (s32[512]{0:T(512)S(1)}, s32[512]{0:T(512)}, u32[]{:S(2)}) copy-start(s32[512]{0:T(512)} %param.23) | copy-start | bytes 6148
  65.3 4.7 %copy-start.10 = (s32[16]{0:T(128)S(1)}, s32[16]{0:T(128)}, u32[]{:S(2)}) copy-start(s32[16]{0:T(128)} %param.25) | copy-start | bytes 196
  65.3 30.7 %copy-start.11 = (s32[64]{0:T(128)S(1)}, s32[64]{0:T(128)}, u32[]{:S(2)}) copy-start(s32[64]{0:T(128)} %param.24) | copy-start | bytes 772
  65.3 40.0 %copy-start.13 = (f32[2304]{0:T(1024)S(1)}, f32[2304]{0:T(1024)}, u32[]{:S(2)}) copy-start(f32[2304]{0:T(1024)} %param.17) | copy-start | bytes 27652
  68.1 104.3 %all-gather.11.cloned.1.call-start = ((), (), s32[]{:S(2)}) async-start(), calls=%async_computation.3 | async-start | bytes 2359296 | tf_op jit(solution)/shard_map/all_gather | solution.py:184
  69.9 178.0 %reduce-scatter.2.cloned.1.call-start = ((), (), s32[]{:S(2)}) async-start(), calls=%async_computation.2 | async-start | bytes 5898240 | tf_op jit(solution)/shard_map/reduce_scatter | solution.py:194
  124.8 6.0 %copy-start.1 = (pred[512,1024]{0,1:T(8,128)(4,1)}, pred[512,1024]{0,1:T(8,128)(4,1)S(1)}, u32[]{:S(2)}) copy-start(pred[512,1024]{0,1:T(8,128)(4,1)S(1)} %and_and_fusion.5) | copy-start | bytes 1572868 | tf_op jit(solution)/shard_map/while
  136.8 6.0 %copy-start.1 = (pred[512,1024]{0,1:T(8,128)(4,1)}, pred[512,1024]{0,1:T(8,128)(4,1)S(1)}, u32[]{:S(2)}) copy-start(pred[512,1024]{0,1:T(8,128)(4,1)S(1)} %and_and_fusion.5) | copy-start | bytes 1572868 | tf_op jit(solution)/shard_map/while
  149.0 6.0 %copy-start.1 = (pred[512,1024]{0,1:T(8,128)(4,1)}, pred[512,1024]{0,1:T(8,128)(4,1)S(1)}, u32[]{:S(2)}) copy-start(pred[512,1024]{0,1:T(8,128)(4,1)S(1)} %and_and_fusion.5) | copy-start | bytes 1572868 | tf_op jit(solution)/shard_map/while
  161.2 6.0 %copy-start.1 = (pred[512,1024]{0,1:T(8,128)(4,1)}, pred[512,1024]{0,1:T(8,128)(4,1)S(1)}, u32[]{:S(2)}) copy-start(pred[512,1024]{0,1:T(8,128)(4,1)S(1)} %and_and_fusion.5) | copy-start | bytes 1572868 | tf_op jit(solution)/shard_map/while
  174.2 2.7 %copy-start.5 = (f32[512,2,256]{2,0,1:T(8,128)S(1)}, f32[512,2,256]{2,0,1:T(8,128)}, u32[]{:S(2)}) copy-start(f32[512,2,256]{2,0,1:T(8,128)} %get-tuple-element.684) | copy-start | bytes 3145732 | tf_op jit(solution)/shard_map/while
  178.8 1.0 copy-start.6
  181.6 2.7 %copy-start.5 = (f32[512,2,256]{2,0,1:T(8,128)S(1)}, f32[512,2,256]{2,0,1:T(8,128)}, u32[]{:S(2)}) copy-start(f32[512,2,256]{2,0,1:T(8,128)} %get-tuple-element.684) | copy-start | bytes 3145732 | tf_op jit(solution)/shard_map/while
  186.2 1.0 copy-start.6
  192.5 56.9 %copy-start.3 = (bf16[128,2304]{1,0:T(8,128)(2,1)S(1)}, bf16[128,2304]{1,0:T(8,128)(2,1)}, u32[]{:S(2)}) copy-start(bf16[128,2304]{1,0:T(8,128)(2,1)} %param.16) | copy-start | bytes 1769476
  192.5 56.9 %copy-start.8 = (f32[2304]{0:T(1024)S(1)}, f32[2304]{0:T(1024)}, u32[]{:S(2)}) copy-start(f32[2304]{0:T(1024)} %param.18) | copy-start | bytes 27652
Sparse Core Ops, SparseCore 0:
  68.3 45.7 all-gather.8
  115.6 28.0 all-gather.10
  192.6 55.2 reduce-scatter.1
